TPU v7x, 32 devices: a whole 2x2x4 slice. The times are simulated.
32 devices in a mesh: band: 8 (over z, y), mode: 4 (over x, core).
Axes of the slice: x: 2, y: 2, z: 4, core: 2. Of those that a mesh axis runs over, the one named last changes fastest.
Arguments:
- velocity: bfloat16 [1, 8192, 1024], P(None, ('band', 'mode')), may hold values from -6 to 6
- radiation_modes: bfloat16 [8192, 1024], P('band', 'mode'), may hold values from -0.125 to 0.125
- resistance: float32 [8, 1024, 1024], P('band', None, 'mode'), as said below
- mode_ranks: int32 [8], P('band'), may hold values from 128 to 1024, as said below
- freq_table: int32 [512], replicated, may hold values from 0 to 511, each once
Outputs:
- adjoint_force: bfloat16 [1, 8192, 1024], P(None, ('band', 'mode'))
Inputs may be any that keep to these rules, and one draw needn't show every extreme that they name: `resistance`: each band's matrix is symmetric. `mode_ranks`: the ranks never fall with the band index; the first band keeps 1024 // 8 modes and the last 1024.
All inputs are finite; a program needn't handle non-finite values.
Results may differ from a plain program's by a relative error of at most 0.015.
Values may be sent and summed in bfloat16 or wider, within the bound.
A program may use at most 64 MiB of HBM per device.

v0:
```python
import math
import jax
import jax.numpy as jnp
from jax import lax
from jax.sharding import PartitionSpec as P


def make_table(freq_table, step_count):
    times = jnp.arange(step_count, dtype=jnp.int32)
    phases = times[:, None] * freq_table[None, :] % step_count
    angles = phases.astype(jnp.float32) * (2.0 * math.pi / step_count)
    norming = 1.0 / math.sqrt(step_count)
    table = jnp.stack([jnp.cos(angles), -jnp.sin(angles)], axis=1) * norming
    return table.astype(jnp.bfloat16)


def add_sources(received):
    return jnp.sum(received, axis=0)


def per_device(velocity, radiation_modes, resistance, mode_ranks, freq_table):
    step_count = velocity.shape[2]
    mode_cols = radiation_modes.shape[1]
    dft_table = make_table(freq_table, step_count)
    spectra = jnp.einsum(
        "wpt,tcf->wpcf", velocity, dft_table, preferred_element_type=jnp.float32
    ).astype(jnp.bfloat16)
    partial_value = jnp.einsum(
        "wpcf,pr->wrcf",
        lax.all_gather(spectra, "mode", axis=1, tiled=True),
        radiation_modes,
        preferred_element_type=jnp.float32,
    )
    coefficients = add_sources(
        lax.all_to_all(
            partial_value[None].astype(jnp.bfloat16),
            "band",
            split_axis=4,
            concat_axis=0,
            tiled=True,
        ).astype(jnp.float32)
    )
    offset = lax.axis_index("mode") * mode_cols
    rank_here = mode_ranks[0]
    kept_mask = (offset + jnp.arange(mode_cols, dtype=jnp.int32) < rank_here).astype(jnp.float32)
    kept_mask = kept_mask[None, :, None, None]
    coefficients = coefficients * kept_mask
    matrix = resistance[0]
    partial_terms = jnp.einsum(
        "ij,wjcf->wicf", matrix, coefficients, precision=lax.Precision.HIGHEST
    )
    forcing = lax.psum_scatter(
        partial_terms.astype(jnp.bfloat16), "mode", scatter_dimension=1, tiled=True
    ).astype(jnp.float32)
    forcing = (2.0 * forcing * kept_mask).astype(jnp.bfloat16)
    collected = lax.all_gather(forcing, "mode", axis=1, tiled=True)
    collected = lax.all_gather(collected, "band", axis=3, tiled=True)
    own_basis = lax.all_to_all(radiation_modes, "mode", split_axis=0, concat_axis=1, tiled=True)
    surface_force = jnp.einsum(
        "pr,wrcf->wpcf", own_basis, collected, preferred_element_type=jnp.float32
    ).astype(jnp.bfloat16)
    history = jnp.einsum(
        "wpcf,tcf->wpt", surface_force, dft_table, preferred_element_type=jnp.float32
    )
    return history.astype(jnp.bfloat16)


def solution(mesh):
    placed = (
        P(None, ("band", "mode"), None),
        P("band", "mode"),
        P("band", None, "mode"),
        P("band"),
        P(),
    )
    return jax.shard_map(
        per_device,
        mesh=mesh,
        in_specs=placed,
        out_specs=P(None, ("band", "mode"), None),
        check_vma=False,
    )
```

profile of v0, /device:TPU:0, one launch (start us, length us, event | category | flops | bytes accessed | tf_op | source)
XLA Modules:
  0.0 158.5 jit_solution(3879735066893673971)
XLA Ops:
  6.5 9.1 %fusion.21 = (f32[1024,1,512]{0,2,1:T(8,128)S(1)}, f32[1024,1,512]{0,2,1:T(8,128)S(1)}) fusion(s32[512]{0:T(512)} %param.9), kind=kLoop, calls=%fused_computation.27 | loop fusion | flops 7864320 | bytes 4196352 | tf_op jit(solution)/shard_map/cos | solution.py:13
  15.7 1.3 copy-done.1
  17.0 0.6 copy-done.2
  17.7 1.6 fusion.13
  19.2 0.0 all-gather.6.cloned.1.call-update
  19.2 25.7 %all-gather.6.cloned.1.call-done = bf16[1024,2,512]{0,2,1:T(8,128)(2,1)} async-done(((bf16[256,2,512]{0,2,1:T(8,128)(2,1)}), bf16[1024,2,512]{0,2,1:T(8,128)(2,1)}) %all-gather.6.cloned.1.call-update) | async-done | bytes 2097168 | tf_op jit(solution)/shard_map/all_gather | solution.py:30
  44.9 2.3 %fusion.14 = bf16[1,1,256,2,512]{2,4,3,1,0:T(8,128)(2,1)S(1)} fusion(bf16[1024,2,512]{0,2,1:T(8,128)(2,1)} %all-gather.6.cloned.1.call-done, bf16[1024,256]{1,0:T(8,128)(2,1)S(1)} %copy-done.3), kind=kOutput, calls=%fused_computation.20 | convolution fusion | flops 537133056 | bytes 3145728 | tf_op jit(solution)/shard_map/wpcf,pr->wrcf/dot_general | solution.py:28
  47.2 1.3 copy.16
  48.6 5.5 %all-to-all-start = ((bf16[1,1,256,2,512]{2,3,1,0,4:T(2,128)(2,1)}), bf16[1,1,256,2,512]{2,3,1,0,4:T(2,128)(2,1)S(1)}, u32[]{:S(2)}, u32[]{:S(2)}) async-start(bf16[1,1,256,2,512]{2,3,1,0,4:T(2,128)(2,1)} %copy.16), calls=%async_computation | async-start | bytes 1048576 | tf_op jit(solution)/shard_map/all_to_all | solution.py:35
  54.1 0.2 reduce-scatter.2.cloned.1.call-start
  55.0 14.0 %all-to-all-done = bf16[1,1,256,2,512]{2,3,1,0,4:T(2,128)(2,1)S(1)} async-done(((bf16[1,1,256,2,512]{2,3,1,0,4:T(2,128)(2,1)}), bf16[1,1,256,2,512]{2,3,1,0,4:T(2,128)(2,1)S(1)}, u32[]{:S(2)}, u32[]{:S(2)}) %all-to-all-start) | async-done | bytes 524320 | tf_op jit(solution)/shard_map/all_to_all | solution.py:35
  69.0 0.5 convert_reduce_fusion
  69.5 1.9 %fusion.19 = bf16[1,1024,2,64]{1,3,2,0:T(8,128)(2,1)} fusion(f32[1,1024,256]{2,1,0:T(8,128)S(1)} %copy-done, f32[256,2,64]{0,1,2:T(2,128)S(1)} %convert_reduce_fusion, f32[256]{0:T(256)S(1)} %fusion.30), kind=kOutput, calls=%fused_computation.24 | convolution fusion | flops 402817024 | bytes 1442816 | tf_op jit(solution)/shard_map/ij,wjcf->wicf/dot_general | solution.py:49
  71.4 0.0 reduce-scatter.2.cloned.1.call-update
  71.4 0.0 all-gather.4.cloned.1.call-start
  71.5 18.3 %reduce-scatter.2.cloned.1.call-done = bf16[1,256,2,64]{1,3,2,0:T(8,128)(2,1)} async-done(((bf16[1,1024,2,64]{1,3,2,0:T(8,128)(2,1)}), bf16[1,256,2,64]{1,3,2,0:T(8,128)(2,1)}) %reduce-scatter.2.cloned.1.call-update) | async-done | bytes 65552 | tf_op jit(solution)/shard_map/reduce_scatter | solution.py:52
  89.7 0.9 multiply_convert_fusion
  90.6 6.2 %all_gather.10 = bf16[1,1024,2,64]{1,3,2,0:T(8,128)(2,1)} all-gather(bf16[1,256,2,64]{1,3,2,0:T(8,128)(2,1)S(1)} %multiply_convert_fusion), channel_id=1, replica_groups=mesh['band'=8,'mode'=4] {'mode'}, dimensions={1}, use_global_device_ids=true | all-gather | bytes 327680 | tf_op jit(solution)/shard_map/all_gather | solution.py:56
  96.8 0.0 all-gather.4.cloned.1.call-update
  96.8 11.2 %all_to_all.28 = bf16[4,256,256]{2,1,0:T(8,128)(2,1)S(1)} all-to-all(bf16[4,256,256]{2,1,0:T(8,128)(2,1)S(1)} %bitcast.57), channel_id=1, replica_groups=mesh['band'=8,'mode'=4] {'mode'}, dimensions={0} | all-to-all | bytes 1048576 | tf_op jit(solution)/shard_map/all_to_all | solution.py:58
  108.1 0.4 copy.18
  108.5 0.4 reshape.162
  108.8 37.2 %all-gather.4.cloned.1.call-done = bf16[1,1024,2,512]{1,3,2,0:T(8,128)(2,1)} async-done(((bf16[1,1024,2,64]{1,3,2,0:T(8,128)(2,1)}), bf16[1,1024,2,512]{1,3,2,0:T(8,128)(2,1)}) %all-gather.4.cloned.1.call-update) | async-done | bytes 2097168 | tf_op jit(solution)/shard_map/all_gather | solution.py:57
  146.1 5.9 %fusion.18 = bf16[1,256,1024]{2,1,0:T(8,128)(2,1)} fusion(bf16[256,1024,1]{1,0,2:T(8,128)(2,1)S(1)} %reshape.162, bf16[1,1024,2,512]{1,3,2,0:T(8,128)(2,1)} %all-gather.4.cloned.1.call-done, f32[1024,1,512]{0,2,1:T(8,128)} %copy-done.2, f32[1024,1,512]{0,2,1:T(8,128)} %copy-done.1), kind=kOutput, calls=%fused_computation.22 | convolution fusion | flops 1077411840 | bytes 7340032 | tf_op jit(solution)/shard_map/wpcf,tcf->wpt/dot_general | solution.py:62
  (11 shorter events, 0.0 us)
Async XLA Ops:
  6.5 62.9 %copy-start = (f32[1,1024,256]{2,1,0:T(8,128)S(1)}, f32[1,1024,256]{2,1,0:T(8,128)}, u32[]{:S(2)}) copy-start(f32[1,1024,256]{2,1,0:T(8,128)} %param.7) | copy-start | bytes 3145732
  6.5 11.1 %copy-start.4 = (bf16[1,256,1024]{2,1,0:T(8,128)(2,1)S(1)}, bf16[1,256,1024]{2,1,0:T(8,128)(2,1)}, u32[]{:S(2)}) copy-start(bf16[1,256,1024]{2,1,0:T(8,128)(2,1)} %param.5) | copy-start | bytes 1572868
  6.5 38.4 %all-gather.6.cloned.1.call-start = ((), (), s32[]{:S(2)}) async-start(), calls=%async_computation.5 | async-start | bytes 2621440 | tf_op jit(solution)/shard_map/all_gather | solution.py:30
  15.7 1.3 copy-start.1
  15.7 1.9 %copy-start.2 = (f32[1024,1,512]{0,2,1:T(8,128)}, f32[1024,1,512]{0,2,1:T(8,128)S(1)}, u32[]{:S(2)}) copy-start(f32[1024,1,512]{0,2,1:T(8,128)S(1)} %get-tuple-element.6) | copy-start | bytes 6291460
  17.7 27.3 %copy-start.3 = (bf16[1024,256]{1,0:T(8,128)(2,1)S(1)}, bf16[1024,256]{1,0:T(8,128)(2,1)}, u32[]{:S(2)}) copy-start(bf16[1024,256]{1,0:T(8,128)(2,1)} %param.6) | copy-start | bytes 1572868
  48.6 20.4 %all-to-all-start = ((bf16[1,1,256,2,512]{2,3,1,0,4:T(2,128)(2,1)}), bf16[1,1,256,2,512]{2,3,1,0,4:T(2,128)(2,1)S(1)}, u32[]{:S(2)}, u32[]{:S(2)}) async-start(bf16[1,1,256,2,512]{2,3,1,0,4:T(2,128)(2,1)} %copy.16), calls=%async_computation | async-start | bytes 1048576 | tf_op jit(solution)/shard_map/all_to_all | solution.py:35
  54.1 35.7 %reduce-scatter.2.cloned.1.call-start = ((), (), s32[]{:S(2)}) async-start(), calls=%async_computation.3 | async-start | bytes 327680 | tf_op jit(solution)/shard_map/reduce_scatter | solution.py:52
  71.4 74.7 %all-gather.4.cloned.1.call-start = ((), (), s32[]{:S(2)}) async-start(), calls=%async_computation.4 | async-start | bytes 2359296 | tf_op jit(solution)/shard_map/all_gather | solution.py:57
Sparse Core Ops, SparseCore 0:
  19.4 25.5 all-gather.5
  71.5 18.1 reduce-scatter.1
  97.0 49.0 all-gather.3
where the time goes:
time: 159 us
  waiting for transfers between devices  95.3 us (60%)
  blocking collectives  17.4 us (11%)
  between operations  13.8 us (9%)
  matrix products  11.7 us (7%)
  other arithmetic  10.5 us (7%)
  starting transfers between devices  5.78 us (4%)
  local copies, waits for them, and re-layouts  4.06 us (3%)
    all_gather x1, waiting for transfers between devices, per_device(): collected = lax.all_gather(collected, 'band', axis=3, tiled=True)  37.2 us
    all_gather x1, waiting for transfers between devices, per_device(): lax.all_gather(spectra, 'mode', axis=1, tiled=True)  25.7 us
    reduce_scatter x1, waiting for transfers between devices, per_device(): lax.psum_scatter(partial_terms.astype(jnp.bfloat16), 'mode', scatter_dime...  18.3 us
    all_to_all x1, waiting for transfers between devices, per_device(): lax.all_to_all(partial_value[None].astype(jnp.bfloat16), 'band', split_ax...  14 us
    all_to_all x1, blocking collectives, per_device(): lax.all_to_all(radiation_modes, 'mode', split_axis=0, concat_axis=1, tile...  11.2 us
    cos x1, other arithmetic, make_table(): table = jnp.stack([jnp.cos(angles), -jnp.sin(angles)], axis=1) * norming  9.14 us
    all_gather x1, blocking collectives, per_device(): collected = lax.all_gather(forcing, 'mode', axis=1, tiled=True)  6.23 us
    dot_general x1, matrix products, per_device(): jnp.einsum('wpcf,tcf->wpt', surface_force, dft_table, preferred_element_t...  5.95 us
  transfers between devices with their start and end apart: 4, of which 4 were waited for; matrix products, arithmetic and copies ran while one was open for 0% of the time, Pallas kernels for 0%

commit v1 on v0

--- a/solution.py
+++ b/solution.py
@@ -54,7 +54,8 @@
     ).astype(jnp.float32)
     forcing = (2.0 * forcing * kept_mask).astype(jnp.bfloat16)
     collected = lax.all_gather(forcing, "mode", axis=1, tiled=True)
-    collected = lax.all_gather(collected, "band", axis=3, tiled=True)
+    mix_clusters = lambda mine, dim_at: jnp.concatenate(lax.all_gather(mine, "band"), dim_at)
+    collected = mix_clusters(collected, 3)
     own_basis = lax.all_to_all(radiation_modes, "mode", split_axis=0, concat_axis=1, tiled=True)
     surface_force = jnp.einsum(
         "pr,wrcf->wpcf", own_basis, collected, preferred_element_type=jnp.float32

time: 159 us -> 160 us (level)
  local copies, waits for them, and re-layouts: 4.06 us -> 6.73 us
    all_gather x0 -> x1, local copies, waits for them, and re-layouts: none -> 1.85 us  [per_device(): lax.all_gather(mine, 'band')]
  transfers between devices with their start and end apart: 4 -> 4, of which waited for: 4 -> 4; matrix products, arithmetic and copies ran while one was open for 0% -> 1% of each run, Pallas kernels for 0% -> 0%
where the time goes in v1:
time: 160 us
  waiting for transfers between devices  94.5 us (59%)
  blocking collectives  17.4 us (11%)
  between operations  13.8 us (9%)
  matrix products  11.2 us (7%)
  other arithmetic  10.5 us (7%)
  local copies, waits for them, and re-layouts  6.73 us (4%)
  starting transfers between devices  5.78 us (4%)
    all_gather x1, waiting for transfers between devices, per_device(): lax.all_gather(mine, 'band')  36.4 us
    all_gather x1, waiting for transfers between devices, per_device(): lax.all_gather(spectra, 'mode', axis=1, tiled=True)  25.7 us
    reduce_scatter x1, waiting for transfers between devices, per_device(): lax.psum_scatter(partial_terms.astype(jnp.bfloat16), 'mode', scatter_dime...  18.3 us
    all_to_all x1, waiting for transfers between devices, per_device(): lax.all_to_all(partial_value[None].astype(jnp.bfloat16), 'band', split_ax...  14 us
    all_to_all x1, blocking collectives, per_device(): lax.all_to_all(radiation_modes, 'mode', split_axis=0, concat_axis=1, tile...  11.2 us
    cos x1, other arithmetic, make_table(): table = jnp.stack([jnp.cos(angles), -jnp.sin(angles)], axis=1) * norming  9.14 us
    all_gather x1, blocking collectives, per_device(): collected = lax.all_gather(forcing, 'mode', axis=1, tiled=True)  6.23 us
    all_to_all x1, starting transfers between devices, per_device(): lax.all_to_all(partial_value[None].astype(jnp.bfloat16), 'band', split_ax...  5.52 us
  transfers between devices with their start and end apart: 4, of which 4 were waited for; matrix products, arithmetic and copies ran while one was open for 1% of the time, Pallas kernels for 0%

profile of v1, /device:TPU:0, one launch (start us, length us, event | category | flops | bytes accessed | tf_op | source)
XLA Modules:
  0.0 159.9 jit_solution(7024196376949628525)
XLA Ops:
  6.5 9.1 %fusion.14 = (f32[1024,1,512]{0,2,1:T(8,128)S(1)}, f32[1024,1,512]{0,2,1:T(8,128)S(1)}) fusion(s32[512]{0:T(512)} %param.9), kind=kLoop, calls=%fused_computation.25 | loop fusion | flops 7864320 | bytes 4196352 | tf_op jit(solution)/shard_map/cos | solution.py:13
  15.7 1.3 copy-done.1
  17.0 0.6 copy-done.2
  17.7 1.6 fusion.8
  19.2 25.7 %all-gather.5.cloned.1.call-done = bf16[1024,2,512]{0,2,1:T(8,128)(2,1)} async-done(((bf16[256,2,512]{0,2,1:T(8,128)(2,1)}), bf16[1024,2,512]{0,2,1:T(8,128)(2,1)}) %all-gather.5.cloned.1.call-update) | async-done | bytes 2097168 | tf_op jit(solution)/shard_map/all_gather | solution.py:30
  44.9 2.3 %fusion.9 = bf16[1,1,256,2,512]{2,4,3,1,0:T(8,128)(2,1)S(1)} fusion(bf16[1024,2,512]{0,2,1:T(8,128)(2,1)} %all-gather.5.cloned.1.call-done, bf16[1024,256]{1,0:T(8,128)(2,1)S(1)} %copy-done.3), kind=kOutput, calls=%fused_computation.18 | convolution fusion | flops 537133056 | bytes 3145728 | tf_op jit(solution)/shard_map/wpcf,pr->wrcf/dot_general | solution.py:28
  47.2 1.3 copy.22
  48.6 5.5 %all-to-all-start = ((bf16[1,1,256,2,512]{2,3,1,0,4:T(2,128)(2,1)}), bf16[1,1,256,2,512]{2,3,1,0,4:T(2,128)(2,1)S(1)}, u32[]{:S(2)}, u32[]{:S(2)}) async-start(bf16[1,1,256,2,512]{2,3,1,0,4:T(2,128)(2,1)} %copy.22), calls=%async_computation | async-start | bytes 1048576 | tf_op jit(solution)/shard_map/all_to_all | solution.py:35
  54.1 0.2 reduce-scatter.2.cloned.1.call-start
  55.0 14.0 %all-to-all-done = bf16[1,1,256,2,512]{2,3,1,0,4:T(2,128)(2,1)S(1)} async-done(((bf16[1,1,256,2,512]{2,3,1,0,4:T(2,128)(2,1)}), bf16[1,1,256,2,512]{2,3,1,0,4:T(2,128)(2,1)S(1)}, u32[]{:S(2)}, u32[]{:S(2)}) %all-to-all-start) | async-done | bytes 524320 | tf_op jit(solution)/shard_map/all_to_all | solution.py:35
  69.0 0.5 convert_reduce_fusion
  69.5 1.9 %fusion.12 = bf16[1,1024,2,64]{1,3,2,0:T(8,128)(2,1)} fusion(f32[1,1024,256]{2,1,0:T(8,128)S(1)} %copy-done, f32[256,2,64]{0,1,2:T(2,128)S(1)} %convert_reduce_fusion, f32[256]{0:T(256)S(1)} %fusion.21), kind=kOutput, calls=%fused_computation.22 | convolution fusion | flops 402817024 | bytes 1442816 | tf_op jit(solution)/shard_map/ij,wjcf->wicf/dot_general | solution.py:49
  71.4 0.0 reduce-scatter.2.cloned.1.call-update
  71.4 0.0 all-gather.7.cloned.1.call-start
  71.5 18.3 %reduce-scatter.2.cloned.1.call-done = bf16[1,256,2,64]{1,3,2,0:T(8,128)(2,1)} async-done(((bf16[1,1024,2,64]{1,3,2,0:T(8,128)(2,1)}), bf16[1,256,2,64]{1,3,2,0:T(8,128)(2,1)}) %reduce-scatter.2.cloned.1.call-update) | async-done | bytes 65552 | tf_op jit(solution)/shard_map/reduce_scatter | solution.py:52
  89.7 0.9 multiply_convert_fusion
  90.6 6.2 %all_gather.13 = bf16[1,1024,2,64]{1,3,2,0:T(8,128)(2,1)} all-gather(bf16[1,256,2,64]{1,3,2,0:T(8,128)(2,1)S(1)} %multiply_convert_fusion), channel_id=1, replica_groups=mesh['band'=8,'mode'=4] {'mode'}, dimensions={1}, use_global_device_ids=true | all-gather | bytes 327680 | tf_op jit(solution)/shard_map/all_gather | solution.py:56
  96.8 0.0 all-gather.7.cloned.1.call-update
  96.8 11.2 %all_to_all.28 = bf16[4,256,256]{2,1,0:T(8,128)(2,1)S(1)} all-to-all(bf16[4,256,256]{2,1,0:T(8,128)(2,1)S(1)} %bitcast.55), channel_id=1, replica_groups=mesh['band'=8,'mode'=4] {'mode'}, dimensions={0} | all-to-all | bytes 1048576 | tf_op jit(solution)/shard_map/all_to_all | solution.py:59
  108.1 0.4 copy.25
  108.5 1.2 reshape.169
  109.7 36.4 %all-gather.7.cloned.1.call-done = bf16[8,1024,2,64]{1,3,2,0:T(8,128)(2,1)} async-done(((bf16[1,1024,2,64]{1,3,2,0:T(8,128)(2,1)}), bf16[8,1024,2,64]{1,3,2,0:T(8,128)(2,1)}) %all-gather.7.cloned.1.call-update) | async-done | bytes 2097168 | tf_op jit(solution)/shard_map/all_gather | solution.py:57
  146.1 1.8 %copy.24 = bf16[8,1024,2,64]{1,3,0,2:T(8,128)(2,1)S(1)} copy(bf16[8,1024,2,64]{1,3,2,0:T(8,128)(2,1)} %all-gather.7.cloned.1.call-done) | data formatting | bytes 4194304 | tf_op jit(solution)/shard_map/all_gather | solution.py:57
  147.9 5.5 %fusion.11 = bf16[1,256,1024]{2,1,0:T(8,128)(2,1)} fusion(bf16[1024,2,512]{0,2,1:T(8,128)(2,1)S(1)} %bitcast.53, bf16[256,1024,1]{1,0,2:T(8,128)(2,1)} %reshape.169, f32[1024,1,512]{0,2,1:T(8,128)} %copy-done.2, f32[1024,1,512]{0,2,1:T(8,128)} %copy-done.1), kind=kOutput, calls=%fused_computation.20 | convolution fusion | flops 1077411840 | bytes 7340032 | tf_op jit(solution)/shard_map/wpcf,tcf->wpt/dot_general | solution.py:63
  (12 shorter events, 0.0 us)
Async XLA Ops:
  6.5 62.9 %copy-start = (f32[1,1024,256]{2,1,0:T(8,128)S(1)}, f32[1,1024,256]{2,1,0:T(8,128)}, u32[]{:S(2)}) copy-start(f32[1,1024,256]{2,1,0:T(8,128)} %param.7) | copy-start | bytes 3145732
  6.5 11.1 %copy-start.4 = (bf16[1,256,1024]{2,1,0:T(8,128)(2,1)S(1)}, bf16[1,256,1024]{2,1,0:T(8,128)(2,1)}, u32[]{:S(2)}) copy-start(bf16[1,256,1024]{2,1,0:T(8,128)(2,1)} %param.5) | copy-start | bytes 1572868
  6.5 38.4 %all-gather.5.cloned.1.call-start = ((), (), s32[]{:S(2)}) async-start(), calls=%async_computation.4 | async-start | bytes 2621440 | tf_op jit(solution)/shard_map/all_gather | solution.py:30
  15.7 1.3 copy-start.1
  15.7 1.9 %copy-start.2 = (f32[1024,1,512]{0,2,1:T(8,128)}, f32[1024,1,512]{0,2,1:T(8,128)S(1)}, u32[]{:S(2)}) copy-start(f32[1024,1,512]{0,2,1:T(8,128)S(1)} %get-tuple-element.6) | copy-start | bytes 6291460
  17.7 27.3 %copy-start.3 = (bf16[1024,256]{1,0:T(8,128)(2,1)S(1)}, bf16[1024,256]{1,0:T(8,128)(2,1)}, u32[]{:S(2)}) copy-start(bf16[1024,256]{1,0:T(8,128)(2,1)} %param.6) | copy-start | bytes 1572868
  48.6 20.4 %all-to-all-start = ((bf16[1,1,256,2,512]{2,3,1,0,4:T(2,128)(2,1)}), bf16[1,1,256,2,512]{2,3,1,0,4:T(2,128)(2,1)S(1)}, u32[]{:S(2)}, u32[]{:S(2)}) async-start(bf16[1,1,256,2,512]{2,3,1,0,4:T(2,128)(2,1)} %copy.22), calls=%async_computation | async-start | bytes 1048576 | tf_op jit(solution)/shard_map/all_to_all | solution.py:35
  54.1 35.7 %reduce-scatter.2.cloned.1.call-start = ((), (), s32[]{:S(2)}) async-start(), calls=%async_computation.3 | async-start | bytes 327680 | tf_op jit(solution)/shard_map/reduce_scatter | solution.py:52
  71.4 74.7 %all-gather.7.cloned.1.call-start = ((), (), s32[]{:S(2)}) async-start(), calls=%async_computation.5 | async-start | bytes 2359296 | tf_op jit(solution)/shard_map/all_gather | solution.py:57
Sparse Core Ops, SparseCore 0:
  19.4 25.5 all-gather.4
  71.5 18.1 reduce-scatter.1
  97.0 49.0 all-gather.6
